TPU v7x, 32 devices: a whole 2x2x4 slice. The times are simulated.
32 devices in a mesh: dp: 16 (over z, y, x), mp: 2 (over core).
Axes of the slice: x: 2, y: 2, z: 4, core: 2. Of those that a mesh axis runs over, the one named last changes fastest.
Arguments:
- residual: bfloat16 [256, 4608], P(None, 'dp'), may hold values from -60 to 60
- norm_gain: float32 [4608], P('dp'), may hold values from 0.25 to 1.75
- query_weight: bfloat16 [4608, 2048], P('dp', 'mp'), may hold values from -2 to 2
- key_weight: bfloat16 [4608, 1024], P('dp', 'mp'), may hold values from -2 to 2
- value_weight: bfloat16 [4608, 1024], P('dp', 'mp'), may hold values from -0.09375 to 0.09375
- out_weight: bfloat16 [2048, 4608], P('mp', 'dp'), may hold values from -1 to 1
- post_gain: float32 [4608], P('dp'), may hold values from 0.25 to 1.75
- encoder_weight: bfloat16 [4608, 8192], P(None, ('dp', 'mp')), may hold values from -0.09375 to 0.09375
- encoder_bias: float32 [8192], P(('dp', 'mp')), may hold values from -3 to 3
- decoder_weight: bfloat16 [8192, 4608], P(('dp', 'mp')), may hold values from -0.125 to 0.125
- decoder_bias: float32 [4608], replicated, may hold values from -3 to 3
Outputs:
- encoder_grad: bfloat16 [4608, 8192], P(None, ('dp', 'mp'))
- encoder_bias_grad: float32 [8192], P(('dp', 'mp'))
- decoder_grad: bfloat16 [8192, 4608], P(('dp', 'mp'))
All inputs are finite; a program needn't handle non-finite values.
Results may differ from a plain program's by a relative error of at most 0.015.
Values may be sent and summed in bfloat16 or wider, within the bound.
No kernel may reach another device: no remote copies, remote signals or barrier semaphores. Data moves between devices by JAX's collectives and lax.ppermute only.
A program may use at most 128 MiB of HBM per device.

v0:
```python
import jax
import jax.numpy as jnp
from jax import lax
from jax.sharding import PartitionSpec as P

HEAD_DIM = 128
epsilon = 1e-06
softcap = 50.0
query_scale = 1.0 / 12.0
rope_base = 10000.0
smoothing = 0.1
penalty = 1.0
loss_weight = 0.0625


def rotate(matrix, positions):
    half_dim = matrix.shape[-1] // 2
    frequency = rope_base ** (-2.0 * jnp.arange(half_dim, dtype=jnp.float32) / matrix.shape[-1])
    angles = positions.astype(jnp.float32)[:, None] * frequency[None, :]
    cosine = jnp.cos(angles)[:, None, :]
    sine_part = jnp.sin(angles)[:, None, :]
    front_half = matrix[..., :half_dim]
    back_half = matrix[..., half_dim:]
    return jnp.concatenate(
        [front_half * cosine - back_half * sine_part, back_half * cosine + front_half * sine_part],
        axis=-1,
    )


def project(summed, square_sum, positions, model_width, query_width, key_width, head_dim):
    inverse = lax.rsqrt(square_sum / model_width + epsilon)
    scaled = summed * inverse[:, None]
    row_count = scaled.shape[0]
    queries = rotate(scaled[:, :query_width].reshape(row_count, -1, head_dim), positions).astype(
        jnp.bfloat16
    )
    keys = rotate(
        scaled[:, query_width : query_width + key_width].reshape(row_count, -1, head_dim), positions
    ).astype(jnp.bfloat16)
    values = (
        scaled[:, query_width + key_width :].reshape(row_count, -1, head_dim).astype(jnp.bfloat16)
    )
    return (queries, keys, values)


def partial_attention(queries, keys, values, query_positions, key_positions):
    row_count, query_heads, head_dim = queries.shape
    key_heads = keys.shape[1]
    grouped = queries.reshape(row_count, key_heads, query_heads // key_heads, head_dim)
    scores = (
        jnp.einsum("rkgd,skd->kgrs", grouped, keys, preferred_element_type=jnp.float32)
        * query_scale
    )
    capped = softcap * jnp.tanh(scores / softcap)
    allowed = query_positions[:, None] >= key_positions[None, :]
    weights = jnp.where(allowed, jnp.exp(capped), 0.0)
    denominator = jnp.sum(weights, axis=3)
    numerator = jnp.einsum(
        "kgrs,skd->rkgd", weights.astype(jnp.bfloat16), values, preferred_element_type=jnp.float32
    )
    return (
        numerator.reshape(row_count, query_heads, head_dim),
        jnp.transpose(denominator, (2, 0, 1)).reshape(row_count, query_heads),
    )


def on_device(
    residual,
    norm_gain,
    query_weight,
    key_weight,
    value_weight,
    out_weight,
    post_gain,
    encoder_weight,
    encoder_bias,
    decoder_weight,
    decoder_bias,
):
    token_count = residual.shape[0]
    model_width = decoder_weight.shape[1]
    head_dim = HEAD_DIM
    query_width = query_weight.shape[1]
    key_width = key_weight.shape[1]
    residual_float = residual.astype(jnp.float32)
    scaled = (residual_float * norm_gain).astype(jnp.bfloat16)
    stacked = jnp.concatenate([query_weight, key_weight, value_weight], axis=1)
    projected_part = jnp.dot(scaled, stacked, preferred_element_type=jnp.float32)
    partial_squares = jnp.sum(residual_float * residual_float, axis=1)
    summed, square_sum = lax.psum((projected_part, partial_squares), "dp")
    positions = jnp.arange(token_count)
    queries, keys, values = project(
        summed, square_sum, positions, model_width, query_width, key_width, head_dim
    )
    numerator, denominator = partial_attention(queries, keys, values, positions, positions)
    attended = (
        (numerator / denominator[:, :, None]).astype(jnp.bfloat16).reshape(token_count, query_width)
    )
    heads_part = jnp.dot(attended, out_weight, preferred_element_type=jnp.float32)
    head_out = lax.psum(heads_part, "mp")
    out_squares = lax.psum(jnp.sum(head_out * head_out, axis=1), "dp")
    normed = head_out * lax.rsqrt(out_squares / model_width + epsilon)[:, None] * post_gain
    hidden_columns = (residual_float + normed).astype(jnp.bfloat16)
    portion = lax.all_gather(hidden_columns, "dp", axis=1, tiled=True)
    preact_sum = jnp.dot(portion, encoder_weight, preferred_element_type=jnp.float32)
    preact_sum, hidden = (preact_sum, portion)
    preact = preact_sum + encoder_bias
    active = smoothing * jax.nn.softplus(preact / smoothing)
    active_low = active.astype(jnp.bfloat16)
    gate_slope = jax.nn.sigmoid(preact / smoothing)
    decoder_norms = jnp.sqrt(
        jnp.sum(jnp.square(decoder_weight.astype(jnp.float32)), axis=1) + epsilon
    )
    activity = jnp.sum(active, axis=0)
    rebuilt_part = jnp.dot(active_low, decoder_weight, preferred_element_type=jnp.float32)
    rebuilt = lax.psum(rebuilt_part, ("dp", "mp"))
    error_low = (rebuilt + decoder_bias - hidden.astype(jnp.float32)).astype(jnp.bfloat16)
    feedback = lax.dot_general(
        error_low, decoder_weight, (((1,), (1,)), ((), ())), preferred_element_type=jnp.float32
    )
    outer_sum = lax.dot_general(
        active_low, error_low, (((0,), (0,)), ((), ())), preferred_element_type=jnp.float32
    )
    grad_active = loss_weight * (2.0 * feedback + penalty * decoder_norms)
    grad_preact = grad_active * gate_slope
    encoder_grad = lax.dot_general(
        hidden,
        grad_preact.astype(jnp.bfloat16),
        (((0,), (0,)), ((), ())),
        preferred_element_type=jnp.float32,
    ).astype(jnp.bfloat16)
    encoder_bias_grad = jnp.sum(grad_preact, axis=0)
    decoder_grad = (
        loss_weight
        * (
            2.0 * outer_sum
            + penalty * (activity / decoder_norms)[:, None] * decoder_weight.astype(jnp.float32)
        )
    ).astype(jnp.bfloat16)
    return (encoder_grad, encoder_bias_grad, decoder_grad)


def solution(mesh):
    placed = (
        P(None, "dp"),
        P("dp"),
        P("dp", "mp"),
        P("dp", "mp"),
        P("dp", "mp"),
        P("mp", "dp"),
        P("dp"),
        P(None, ("dp", "mp")),
        P(("dp", "mp")),
        P(("dp", "mp"), None),
        P(),
    )
    return jax.shard_map(
        on_device,
        mesh=mesh,
        in_specs=placed,
        out_specs=(P(None, ("dp", "mp")), P(("dp", "mp")), P(("dp", "mp"), None)),
        check_vma=False,
    )
```

profile of v0, /device:TPU:0, one launch (start us, length us, event | category | flops | bytes accessed | tf_op | source)
XLA Modules:
  0.0 448.3 jit_solution(4388165543059884381)
XLA Ops:
  7.2 0.0 copy-start
  7.2 0.0 all-reduce.4.cloned.1.call-start
  7.2 3.6 fusion.4
  10.9 0.0 all-reduce.4.cloned.1.call-update
  10.9 0.0 all-reduce.6.cloned.1.call-start
  10.9 0.1 fusion.21
  11.0 44.4 %psum.36 = f32[256]{0:T(256)S(1)} all-reduce(f32[256]{0:T(256)S(1)} %fusion.21), channel_id=1, replica_groups=mesh['dp'=16,'mp'=2] {'dp'}, use_global_device_ids=true, to_apply=%region_2.0 | all-reduce | flops 256 | bytes 2048 | tf_op jit(solution)/shard_map/psum | solution.py:90
  55.4 0.7 iota_compare_fusion
  56.1 1.3 multiply_cosine_fusion
  57.4 85.9 %all-reduce.4.cloned.1.call-done = f32[256,2048]{1,0:T(8,128)} async-done(((f32[256,2048]{1,0:T(8,128)}), f32[256,2048]{1,0:T(8,128)}) %all-reduce.4.cloned.1.call-update) | async-done | bytes 2097168 | tf_op jit(solution)/shard_map/psum | solution.py:90
  143.2 1.8 broadcast_multiply_fusion
  145.1 1.0 slice_bitcast_fusion
  146.1 0.8 slice.42
  146.9 0.2 reshape.99
  147.1 1.1 fusion.36
  148.2 0.1 copy-done.4
  148.3 0.2 copy.28
  148.5 0.5 subtract_convert_fusion.1
  149.0 0.9 copy.16
  149.9 0.9 copy.17
  150.8 1.8 copy.25
  152.6 1.1 subtract_convert_fusion.2
  153.7 3.3 fusion.37
  157.0 1.6 fusion.15
  158.6 0.0 copy-start.12
  158.6 0.0 copy-start.13
  158.6 0.1 fusion.14
  158.7 1.0 fusion.39
  159.8 0.0 all-reduce.6.cloned.1.call-update
  159.8 0.0 all-gather.2.cloned.1.call-start
  159.8 17.8 %all-reduce.6.cloned.1.call-done = f32[256,288]{0,1:T(8,128)} async-done(((f32[256,288]{0,1:T(8,128)}), f32[256,288]{0,1:T(8,128)}) %all-reduce.6.cloned.1.call-update) | async-done | bytes 294928 | tf_op jit(solution)/shard_map/psum | solution.py:100
  177.6 1.0 multiply_reduce_fusion
  178.6 42.0 %psum.38 = f32[256]{0:T(256)S(1)} all-reduce(f32[256]{0:T(256)S(1)} %multiply_reduce_fusion), channel_id=1, replica_groups=mesh['dp'=16,'mp'=2] {'dp'}, use_global_device_ids=true, to_apply=%region_6.7 | all-reduce | flops 256 | bytes 2048 | tf_op jit(solution)/shard_map/psum | solution.py:101
  220.6 1.7 fusion.22
  222.3 0.0 all-gather.2.cloned.1.call-update
  222.4 0.2 all-reduce.8.cloned.1.call-start
  222.6 58.1 %all-gather.2.cloned.1.call-done = bf16[256,4608]{0,1:T(8,128)(2,1)} async-done(((bf16[256,288]{0,1:T(8,128)(2,1)}), bf16[256,4608]{0,1:T(8,128)(2,1)}) %all-gather.2.cloned.1.call-update) | async-done | bytes 2359312 | tf_op jit(solution)/shard_map/all_gather | solution.py:104
  280.7 2.8 fusion.29
  283.5 3.3 fusion.34
  286.8 0.0 all-reduce.8.cloned.1.call-update
  286.8 0.0 copy-start.11
  286.8 2.2 fusion.3
  289.0 141.6 %all-reduce.8.cloned.1.call-done = f32[256,4608]{0,1:T(8,128)} async-done(((f32[256,4608]{0,1:T(8,128)}), f32[256,4608]{0,1:T(8,128)}) %all-reduce.8.cloned.1.call-update) | async-done | bytes 4718608 | tf_op jit(solution)/shard_map/psum | solution.py:116
  430.6 4.2 subtract_convert_fusion
  434.9 3.1 fusion.2
  438.0 1.4 fusion.38
  439.4 0.3 copy-done.1
  439.6 2.2 convolution_convert_fusion
  (29 shorter events, 0.1 us)
Async XLA Ops:
  7.2 273.5 %copy-start = (bf16[4608,256]{1,0:T(8,128)(2,1)S(1)}, bf16[4608,256]{1,0:T(8,128)(2,1)}, u32[]{:S(2)}) copy-start(bf16[4608,256]{1,0:T(8,128)(2,1)} %param.18) | copy-start | bytes 7077892
  7.2 3.8 copy-start.6
  7.2 136.0 %all-reduce.4.cloned.1.call-start = ((), (), s32[]{:S(2)}) async-start(), calls=%async_computation | async-start | bytes 4194304 | tf_op jit(solution)/shard_map/psum | solution.py:90
  10.9 166.7 %all-reduce.6.cloned.1.call-start = ((), (), s32[]{:S(2)}) async-start(), calls=%async_computation.1 | async-start | bytes 589824 | tf_op jit(solution)/shard_map/psum | solution.py:100
  147.1 1.2 copy-start.4
  147.1 1.4 copy-start.7
  147.1 1.4 copy-start.8
  148.5 4.1 copy-start.5
  153.7 3.3 copy-start.9
  157.0 1.7 copy-start.10
  158.6 62.0 %copy-start.12 = (f32[288]{0:T(512)S(1)}, f32[288]{0:T(512)}, u32[]{:S(2)}) copy-start(f32[288]{0:T(512)} %param.17) | copy-start | bytes 3460
  158.6 122.1 %copy-start.13 = (f32[256]{0:T(256)S(1)}, f32[256]{0:T(256)}, u32[]{:S(2)}) copy-start(f32[256]{0:T(256)} %param.19) | copy-start | bytes 3076
  159.8 120.9 %all-gather.2.cloned.1.call-start = ((), (), s32[]{:S(2)}) async-start(), calls=%async_computation.2 | async-start | bytes 2506752 | tf_op jit(solution)/shard_map/all_gather | solution.py:104
  222.4 208.3 %all-reduce.8.cloned.1.call-start = ((), (), s32[]{:S(2)}) async-start(), calls=%async_computation.3 | async-start | bytes 9437184 | tf_op jit(solution)/shard_map/psum | solution.py:116
  280.7 2.8 copy-start.2
  286.8 143.8 %copy-start.11 = (f32[4608]{0:T(1024)S(1)}, f32[4608]{0:T(1024)}, u32[]{:S(2)}) copy-start(f32[4608]{0:T(1024)} %param.21) | copy-start | bytes 55300
  430.6 4.3 copy-start.3
  438.0 1.7 copy-start.1
Sparse Core Ops, SparseCore 0:
  14.1 129.1 all-reduce.3
  159.9 17.6 all-reduce.5
  222.5 58.1 all-gather.1
  287.1 143.4 all-reduce.7
where the time goes:
time: 449 us; the launch traced here: 448 us
  waiting for transfers between devices  303 us (67%)
  blocking collectives  86.3 us (19%)
  matrix products  22.3 us (5%)
  other arithmetic  14.7 us (3%)
  between operations  14 us (3%)
  local copies, waits for them, and re-layouts  7.29 us (2%)
    psum x1, waiting for transfers between devices, on_device(): rebuilt = lax.psum(rebuilt_part, ('dp', 'mp'))  142 us
    psum x1, waiting for transfers between devices, on_device(): summed, square_sum = lax.psum((projected_part, partial_squares), 'dp')  85.9 us
    all_gather x1, waiting for transfers between devices, on_device(): portion = lax.all_gather(hidden_columns, 'dp', axis=1, tiled=True)  58.1 us
    psum x1, blocking collectives, on_device(): summed, square_sum = lax.psum((projected_part, partial_squares), 'dp')  44.4 us
    psum x1, blocking collectives, on_device(): out_squares = lax.psum(jnp.sum(head_out * head_out, axis=1), 'dp')  42 us
    psum x1, waiting for transfers between devices, on_device(): head_out = lax.psum(heads_part, 'mp')  17.8 us
  transfers between devices with their start and end apart: 4, of which 4 were waited for; matrix products, arithmetic and copies ran while one was open for 1% of the time, Pallas kernels for 0%

commit v1 on v0

--- a/solution.py
+++ b/solution.py
@@ -113,7 +113,7 @@
     )
     activity = jnp.sum(active, axis=0)
     rebuilt_part = jnp.dot(active_low, decoder_weight, preferred_element_type=jnp.float32)
-    rebuilt = lax.psum(rebuilt_part, ("dp", "mp"))
+    rebuilt = lax.psum(lax.psum(rebuilt_part, "mp"), "dp")
     error_low = (rebuilt + decoder_bias - hidden.astype(jnp.float32)).astype(jnp.bfloat16)
     feedback = lax.dot_general(
         error_low, decoder_weight, (((1,), (1,)), ((), ())), preferred_element_type=jnp.float32

time: 449 us -> 520 us (1.16)
  waiting for transfers between devices: 303 us -> 374 us
    psum x1 -> x2, waiting for transfers between devices: 142 us -> 212 us  [on_device(): rebuilt = lax.psum(lax.psum(rebuilt_part, 'mp'), 'dp')]
  transfers between devices with their start and end apart: 4 -> 5, of which waited for: 4 -> 5; matrix products, arithmetic and copies ran while one was open for 1% -> 1% of each run, Pallas kernels for 0% -> 0%
where the time goes in v1:
time: 520 us; the launch traced here: 519 us
  waiting for transfers between devices  374 us (72%)
  blocking collectives  86.3 us (17%)
  matrix products  22.3 us (4%)
  other arithmetic  14.7 us (3%)
  between operations  14 us (3%)
  local copies, waits for them, and re-layouts  7.29 us (1%)
    psum x2, waiting for transfers between devices, on_device(): rebuilt = lax.psum(lax.psum(rebuilt_part, 'mp'), 'dp')  212 us
    psum x1, waiting for transfers between devices, on_device(): summed, square_sum = lax.psum((projected_part, partial_squares), 'dp')  85.9 us
    all_gather x1, waiting for transfers between devices, on_device(): portion = lax.all_gather(hidden_columns, 'dp', axis=1, tiled=True)  58.3 us
    psum x1, blocking collectives, on_device(): summed, square_sum = lax.psum((projected_part, partial_squares), 'dp')  44.4 us
    psum x1, blocking collectives, on_device(): out_squares = lax.psum(jnp.sum(head_out * head_out, axis=1), 'dp')  42 us
    psum x1, waiting for transfers between devices, on_device(): head_out = lax.psum(heads_part, 'mp')  17.8 us
  transfers between devices with their start and end apart: 5, of which 5 were waited for; matrix products, arithmetic and copies ran while one was open for 1% of the time, Pallas kernels for 0%

profile of v1, /device:TPU:0, one launch (start us, length us, event | category | flops | bytes accessed | tf_op | source)
XLA Modules:
  0.0 519.2 jit_solution(12731090498127655229)
XLA Ops:
  7.2 0.0 copy-start
  7.2 0.0 all-reduce.5.cloned.1.call-start
  7.2 3.6 fusion.4
  10.9 0.0 all-reduce.5.cloned.1.call-update
  10.9 0.0 all-reduce.7.cloned.1.call-start
  10.9 0.1 fusion.21
  11.0 44.4 %psum.43 = f32[256]{0:T(256)S(1)} all-reduce(f32[256]{0:T(256)S(1)} %fusion.21), channel_id=1, replica_groups=mesh['dp'=16,'mp'=2] {'dp'}, use_global_device_ids=true, to_apply=%region_2.0 | all-reduce | flops 256 | bytes 2048 | tf_op jit(solution)/shard_map/psum | solution.py:90
  55.4 0.7 iota_compare_fusion
  56.1 1.3 multiply_cosine_fusion
  57.4 85.9 %all-reduce.5.cloned.1.call-done = f32[256,2048]{1,0:T(8,128)} async-done(((f32[256,2048]{1,0:T(8,128)}), f32[256,2048]{1,0:T(8,128)}) %all-reduce.5.cloned.1.call-update) | async-done | bytes 2097168 | tf_op jit(solution)/shard_map/psum | solution.py:90
  143.2 1.8 broadcast_multiply_fusion
  145.1 1.0 slice_bitcast_fusion
  146.1 0.8 slice.42
  146.9 0.2 reshape.99
  147.1 1.1 fusion.36
  148.2 0.1 copy-done.4
  148.3 0.2 copy.28
  148.5 0.5 subtract_convert_fusion.1
  149.0 0.9 copy.16
  149.9 0.9 copy.17
  150.8 1.8 copy.25
  152.6 1.1 subtract_convert_fusion.2
  153.7 3.3 fusion.37
  157.0 1.6 fusion.15
  158.6 0.1 fusion.14
  158.7 1.0 fusion.39
  159.8 0.0 all-reduce.7.cloned.1.call-update
  159.8 0.0 all-gather.2.cloned.1.call-start
  159.8 17.8 %all-reduce.7.cloned.1.call-done = f32[256,288]{0,1:T(8,128)} async-done(((f32[256,288]{0,1:T(8,128)}), f32[256,288]{0,1:T(8,128)}) %all-reduce.7.cloned.1.call-update) | async-done | bytes 294928 | tf_op jit(solution)/shard_map/psum | solution.py:100
  177.6 1.0 multiply_reduce_fusion
  178.6 42.0 %psum.45 = f32[256]{0:T(256)S(1)} all-reduce(f32[256]{0:T(256)S(1)} %multiply_reduce_fusion), channel_id=1, replica_groups=mesh['dp'=16,'mp'=2] {'dp'}, use_global_device_ids=true, to_apply=%region_6.7 | all-reduce | flops 256 | bytes 2048 | tf_op jit(solution)/shard_map/psum | solution.py:101
  220.6 1.7 fusion.22
  222.3 0.0 all-gather.2.cloned.1.call-update
  222.4 0.0 all-reduce.9.cloned.1.call-start
  222.4 58.3 %all-gather.2.cloned.1.call-done = bf16[256,4608]{0,1:T(8,128)(2,1)} async-done(((bf16[256,288]{0,1:T(8,128)(2,1)}), bf16[256,4608]{0,1:T(8,128)(2,1)}) %all-gather.2.cloned.1.call-update) | async-done | bytes 2359312 | tf_op jit(solution)/shard_map/all_gather | solution.py:104
  280.7 2.8 fusion.29
  283.5 3.3 fusion.34
  286.8 0.0 all-reduce.9.cloned.1.call-update
  286.8 0.2 all-reduce.11.cloned.1.call-start
  287.0 27.9 %all-reduce.9.cloned.1.call-done = f32[256,4608]{0,1:T(8,128)} async-done(((f32[256,4608]{0,1:T(8,128)}), f32[256,4608]{0,1:T(8,128)}) %all-reduce.9.cloned.1.call-update) | async-done | bytes 4718608 | tf_op jit(solution)/shard_map/psum | solution.py:116
  314.9 0.0 all-reduce.11.cloned.1.call-update
  314.9 2.2 fusion.3
  317.2 184.3 %all-reduce.11.cloned.1.call-done = f32[256,4608]{0,1:T(8,128)} async-done(((f32[256,4608]{0,1:T(8,128)}), f32[256,4608]{0,1:T(8,128)}) %all-reduce.11.cloned.1.call-update) | async-done | bytes 4718608 | tf_op jit(solution)/shard_map/psum | solution.py:116
  501.4 4.2 subtract_convert_fusion
  505.7 3.1 fusion.2
  508.8 1.4 fusion.38
  510.2 0.3 copy-done.1
  510.4 2.2 convolution_convert_fusion
  (32 shorter events, 0.1 us)
Async XLA Ops:
  7.2 273.5 %copy-start = (bf16[4608,256]{1,0:T(8,128)(2,1)S(1)}, bf16[4608,256]{1,0:T(8,128)(2,1)}, u32[]{:S(2)}) copy-start(bf16[4608,256]{1,0:T(8,128)(2,1)} %param.18) | copy-start | bytes 7077892
  7.2 3.8 copy-start.6
  7.2 136.0 %all-reduce.5.cloned.1.call-start = ((), (), s32[]{:S(2)}) async-start(), calls=%async_computation | async-start | bytes 4194304 | tf_op jit(solution)/shard_map/psum | solution.py:90
  10.9 166.7 %all-reduce.7.cloned.1.call-start = ((), (), s32[]{:S(2)}) async-start(), calls=%async_computation.1 | async-start | bytes 589824 | tf_op jit(solution)/shard_map/psum | solution.py:100
  147.1 1.2 copy-start.4
  147.1 1.4 copy-start.7
  147.1 1.4 copy-start.8
  148.5 4.1 copy-start.5
  153.7 3.3 copy-start.9
  157.0 1.7 copy-start.10
  158.6 62.0 %copy-start.12 = (f32[288]{0:T(512)S(1)}, f32[288]{0:T(512)}, u32[]{:S(2)}) copy-start(f32[288]{0:T(512)} %param.17) | copy-start | bytes 3460
  158.6 122.1 %copy-start.13 = (f32[256]{0:T(256)S(1)}, f32[256]{0:T(256)}, u32[]{:S(2)}) copy-start(f32[256]{0:T(256)} %param.19) | copy-start | bytes 3076
  159.8 120.9 %all-gather.2.cloned.1.call-start = ((), (), s32[]{:S(2)}) async-start(), calls=%async_computation.2 | async-start | bytes 2506752 | tf_op jit(solution)/shard_map/all_gather | solution.py:104
  222.4 92.5 %all-reduce.9.cloned.1.call-start = ((), (), s32[]{:S(2)}) async-start(), calls=%async_computation.3 | async-start | bytes 9437184 | tf_op jit(solution)/shard_map/psum | solution.py:116
  280.7 2.8 copy-start.2
  286.8 214.6 %all-reduce.11.cloned.1.call-start = ((), (), s32[]{:S(2)}) async-start(), calls=%async_computation.4 | async-start | bytes 9437184 | tf_op jit(solution)/shard_map/psum | solution.py:116
  314.9 186.5 %copy-start.11 = (f32[4608]{0:T(1024)S(1)}, f32[4608]{0:T(1024)}, u32[]{:S(2)}) copy-start(f32[4608]{0:T(1024)} %param.21) | copy-start | bytes 55300
  501.4 4.3 copy-start.3
  508.8 1.7 copy-start.1
Sparse Core Ops, SparseCore 0:
  14.1 129.1 all-reduce.4
  159.9 17.6 all-reduce.6
  222.5 58.1 all-gather.1
  286.9 27.9 all-reduce.8
  320.5 180.9 all-reduce.10
